TPU v7x, 256 devices: a whole 4x4x8 slice. The times are simulated.
256 devices in a mesh: lat: 32 (over z_hi, y, core), chan: 8 (over z_lo, x).
Axes of the slice: x: 4, y: 4, z: 8 (z_hi: 4, z_lo: 2; z = z_hi * 2 + z_lo), core: 2. Of those that a mesh axis runs over, the one named last changes fastest.
Arguments:
- fields: float32 [256, 900, 768], P(('lat', 'chan')), may hold values from -6 to 6
- first_gain: float32 [768], replicated, may hold values from 0.5 to 1.5
- first_shift: float32 [768], replicated, may hold values from -1.5 to 1.5
- filter_one: float32 [8, 2, 96, 96], P('chan'), may hold values from -0.4375 to 0.4375
- filter_one_bias: float32 [8, 2, 96], P('chan'), may hold values from -2.5 to 2.5
- filter_two: float32 [8, 2, 96, 96], P('chan'), may hold values from -0.4375 to 0.4375
- filter_two_bias: float32 [8, 2, 96], P('chan'), may hold values from -2.5 to 2.5
- second_gain: float32 [768], replicated, may hold values from 0.5 to 1.5
- second_shift: float32 [768], replicated, may hold values from -1.5 to 1.5
- dense_weights: bfloat16 [3072, 2, 768], P(('lat', 'chan')), may hold values from -0.21875 to 0.21875
- dense_bias: bfloat16 [3072], P(('lat', 'chan')), may hold values from -2.5 to 2.5
- output_bias: float32 [768], replicated, may hold values from -1.5 to 1.5
Outputs:
- block_output: float32 [256, 900, 768], P(('lat', 'chan'))
All inputs are finite; a program needn't handle non-finite values.
Results may differ from a plain program's by a relative error of at most 0.0025.
Values may be sent and summed in bfloat16 or wider, within the bound.
No kernel may reach another device: no remote copies, remote signals or barrier semaphores. Data moves between devices by JAX's collectives and lax.ppermute only.
A program may use at most 128 MiB of HBM per device.

v0:
```python
import jax
import jax.numpy as jnp
from jax import lax
from jax.sharding import PartitionSpec as P

KW = 256
exact_mode = lax.Precision.HIGHEST
norm_eps = 1e-05
shrink_level = 0.01
two_pi = 6.283185307179586


def layer_norm(values, gain_terms, shift_terms):
    mean_value = jnp.mean(values, axis=-1, keepdims=True)
    centered = values - mean_value
    variance = jnp.mean(centered * centered, axis=-1, keepdims=True)
    return centered * lax.rsqrt(variance + norm_eps) * gain_terms + shift_terms


def soft_shrink(values):
    return jnp.sign(values) * jnp.maximum(jnp.abs(values) - shrink_level, 0.0)


def mixing_matrix(weight):
    real_weight = weight[:, 0]
    imag_weight = weight[:, 1]
    return jnp.stack(
        [jnp.stack([real_weight, imag_weight]), jnp.stack([-imag_weight, real_weight])]
    )


def complex_layer(spectrum, weight, bias_terms):
    product = jnp.einsum(
        "hakni,abnio->hbkno", spectrum, mixing_matrix(weight), precision=exact_mode
    )
    return product + jnp.transpose(bias_terms, (1, 0, 2))[None, :, None]


def per_device(
    fields,
    first_gain,
    first_shift,
    filter_one,
    filter_one_bias,
    filter_two,
    filter_two_bias,
    second_gain,
    second_shift,
    dense_weights,
    dense_bias,
    output_bias,
):
    row_count, width_count, channels = fields.shape
    lat_count = lax.axis_size("lat")
    chan_count = lax.axis_size("chan")
    height = row_count * lat_count * chan_count
    block_size = filter_one.shape[-1]
    local_blocks = filter_one.shape[0]
    local_modes = KW // lat_count
    normed_in = layer_norm(fields, first_gain, first_shift)
    lon_index = jnp.arange(width_count, dtype=jnp.int32)
    mode_index = jnp.arange(KW, dtype=jnp.int32)
    lon_angle = (
        two_pi
        / width_count
        * (lon_index[:, None] * mode_index[None, :] % width_count).astype(jnp.float32)
    )
    forward_lon = jnp.stack([jnp.cos(lon_angle), -jnp.sin(lon_angle)], axis=1) * width_count ** (
        -0.5
    )
    lon_modes = jnp.einsum("rwc,wak->rakc", normed_in, forward_lon, precision=exact_mode)
    moved = lax.all_to_all(
        lax.all_to_all(lon_modes, "lat", split_axis=2, concat_axis=0, tiled=True),
        "chan",
        split_axis=3,
        concat_axis=0,
        tiled=True,
    )
    position = jnp.arange(height, dtype=jnp.int32)
    true_row = (
        position // row_count % lat_count * chan_count + position // (row_count * lat_count)
    ) * row_count + position % row_count
    lat_index = jnp.arange(height, dtype=jnp.int32)
    forward_angle = (
        two_pi / height * (true_row[:, None] * lat_index[None, :] % height).astype(jnp.float32)
    )
    cos_forward = jnp.cos(forward_angle)
    sin_forward = jnp.sin(forward_angle)
    forward_lat = jnp.stack(
        [
            jnp.stack([cos_forward, -sin_forward], axis=1),
            jnp.stack([sin_forward, cos_forward], axis=1),
        ],
        axis=1,
    ) * height ** (-0.5)
    flat_moved = moved.reshape(height, 2, local_modes * moved.shape[3])
    spectrum = jnp.einsum("pax,pabm->mbx", flat_moved, forward_lat, precision=exact_mode)
    spectrum = spectrum.reshape(height, 2, local_modes, local_blocks, block_size)
    first_out = jnp.maximum(complex_layer(spectrum, filter_one, filter_one_bias), 0.0)
    second_out = soft_shrink(complex_layer(first_out, filter_two, filter_two_bias))
    back_angle = (
        two_pi / height * (lat_index[:, None] * lat_index[None, :] % height).astype(jnp.float32)
    )
    cos_back = jnp.cos(back_angle)
    sin_back = jnp.sin(back_angle)
    inverse_lat = jnp.stack(
        [jnp.stack([cos_back, sin_back], axis=1), jnp.stack([-sin_back, cos_back], axis=1)], axis=1
    ) * height ** (-0.5)
    lat_back = jnp.einsum(
        "max,mabh->hbx", second_out.reshape(height, 2, -1), inverse_lat, precision=exact_mode
    )
    lat_back = lat_back.reshape(height, 2, local_modes, -1)
    returned = lax.all_to_all(
        lax.all_to_all(lat_back, "lat", split_axis=0, concat_axis=2, tiled=True),
        "chan",
        split_axis=0,
        concat_axis=3,
        tiled=True,
    )
    mode_factor = jnp.where(mode_index == 0, 1.0, 2.0).astype(jnp.float32) * width_count ** (-0.5)
    inverse_lon = jnp.stack(
        [jnp.cos(lon_angle).T * mode_factor[:, None], -jnp.sin(lon_angle).T * mode_factor[:, None]]
    )
    filtered = jnp.einsum("rakc,akw->rwc", returned, inverse_lon, precision=exact_mode) + normed_in
    summed = filtered + fields
    token_count = row_count * width_count
    flat_normed = (
        layer_norm(summed, second_gain, second_shift)
        .astype(jnp.bfloat16)
        .reshape(token_count, channels)
    )
    weight_block = lax.all_gather(dense_weights, ("lat", "chan"), axis=0, tiled=True)
    bias_block = lax.all_gather(dense_bias, ("lat", "chan"), axis=0, tiled=True)
    pre_act = lax.dot_general(
        flat_normed,
        weight_block[:, 0, :],
        (((1,), (1,)), ((), ())),
        preferred_element_type=jnp.float32,
    ) + bias_block.astype(jnp.float32)
    hidden = jax.nn.gelu(pre_act, approximate=False).astype(jnp.bfloat16)
    dense_out = jnp.dot(hidden, weight_block[:, 1, :], preferred_element_type=jnp.float32)
    return summed + (dense_out + output_bias).reshape(row_count, width_count, channels)


def solution(mesh):
    placed = (
        P(("lat", "chan"), None, None),
        P(),
        P(),
        P("chan", None, None, None),
        P("chan", None, None),
        P("chan", None, None, None),
        P("chan", None, None),
        P(),
        P(),
        P(("lat", "chan"), None, None),
        P(("lat", "chan")),
        P(),
    )
    return jax.shard_map(
        per_device,
        mesh=mesh,
        in_specs=placed,
        out_specs=P(("lat", "chan"), None, None),
        check_vma=False,
    )
```

profile of v0, /device:TPU:99, one launch (start us, length us, event | category | flops | bytes accessed | tf_op | source)
XLA Modules:
  0.0 880.4 jit_solution(15925368327343979689)
XLA Ops:
  6.5 0.0 all-gather.2.cloned.1.call-start
  6.5 0.7 all-gather.2.cloned.1.call-update
  7.3 4.7 reduce_sum.36
  12.0 0.0 copy-start.12
  12.0 0.0 copy-start.13
  12.0 3.8 sine_negate_fusion
  15.8 0.4 multiply_reduce_fusion.1
  16.2 0.0 copy-done.12
  16.2 0.0 copy-done.13
  16.3 6.4 fusion.34
  22.7 1.2 copy.106
  23.9 49.0 %all_to_all.66 = f32[1,2,256,768]{3,1,0,2:T(2,128)} all-to-all(f32[1,2,256,768]{3,1,0,2:T(2,128)S(1)} %copy.106), channel_id=1, replica_groups=mesh['lat'=32,'chan'=8] {'lat'}, dimensions={2} | all-to-all | bytes 3145728 | tf_op jit(solution)/shard_map/all_to_all | solution.py:73
  72.9 6.5 copy.107
  79.4 5.9 bitcast_bitcast_fusion
  85.3 7.6 reshape.513
  93.0 6.6 all-to-all-start.1
  99.6 0.1 copy.135
  99.7 0.1 copy.134
  99.8 0.0 copy-done.9
  99.8 0.1 copy.133
  99.9 0.1 copy.132
  100.0 0.7 maximum_bitcast_fusion.8
  100.7 1.0 fusion.92
  101.7 1.0 fusion.88
  102.8 1.0 fusion.93
  103.8 1.1 maximum_bitcast_fusion.2
  104.9 0.9 maximum_bitcast_fusion
  105.8 14.5 %all-to-all-done.1 = f32[8,1,49152]{2,1,0:T(1,128)} async-done(((f32[8,1,49152]{2,1,0:T(1,128)}), f32[8,1,49152]{2,1,0:T(1,128)}, u32[]{:S(2)}, u32[]{:S(2)}) %all-to-all-start.1) | async-done | bytes 1572896 | tf_op jit(solution)/shard_map/all_to_all | solution.py:72
  120.2 0.6 broadcast.663
  120.8 6.9 reduce.4
  127.7 6.2 reshape.514
  133.9 5.9 copy.108
  139.8 3.0 reshape.501
  142.8 0.0 copy-start.10
  142.8 5.6 convolution_bitcast_fusion.1
  148.4 3.0 copy.109
  151.5 3.0 fusion.29
  154.5 2.0 maximum_multiply_fusion.2
  156.6 3.9 convolution_bitcast_fusion
  160.4 3.0 copy.113
  163.5 2.9 copy.114
  166.4 56.5 %all_to_all.67 = f32[256,2,8,96]{3,2,1,0:T(8,128)S(1)} all-to-all(f32[256,2,8,96]{3,2,1,0:T(8,128)} %copy.114), channel_id=1, replica_groups=mesh['lat'=32,'chan'=8] {'lat'}, dimensions={0} | all-to-all | bytes 3145728 | tf_op jit(solution)/shard_map/all_to_all | solution.py:114
  222.8 1.5 copy.180
  224.4 2.8 copy.116
  227.2 5.3 all-to-all-start.3
  232.5 0.2 dynamic-update-slice
  232.8 84.4 %all-reduce = bf16[3072]{0:T(1024)(128)(2,1)S(1)} all-reduce(bf16[3072]{0:T(1024)(128)(2,1)S(1)} %dynamic-update-slice), channel_id=1, replica_groups=mesh['lat'=32,'chan'=8] {'lat','chan'}, use_global_device_ids=true, to_apply=%add | all-reduce | flops 3072 | bytes 12288
  317.2 4.9 cosine_multiply_fusion
  322.1 0.0 all-to-all-done.3
  322.1 1.6 copy.117
  323.8 0.3 copy-done.5
  324.1 5.3 fusion.140
  329.4 1.5 copy-done.1
  330.9 0.5 multiply_reduce_fusion
  331.4 0.0 copy-start.14
  331.4 0.0 copy-start.15
  331.4 480.4 %all-gather.2.cloned.1.call-done = bf16[3072,2,768]{2,1,0:T(2,128)(2,1)} async-done(((bf16[12,2,768]{2,1,0:T(2,128)(2,1)}), bf16[3072,2,768]{2,1,0:T(2,128)(2,1)}) %all-gather.2.cloned.1.call-update) | async-done | bytes 9437200 | tf_op jit(solution)/shard_map/all_gather | solution.py:132
  811.8 18.4 %fusion.137 = (bf16[3072,1,768]{2,1,0:T(2,128)(2,1)S(1)}, bf16[3072,1,768]{2,1,0:T(2,128)(2,1)S(1)}) fusion(bf16[3072,2,768]{2,1,0:T(2,128)(2,1)} %all-gather.2.cloned.1.call-done), kind=kLoop, calls=%fused_computation.181 | loop fusion | bytes 18874368 | tf_op jit(solution)/shard_map/slice | solution.py:136
  830.2 0.0 copy-start.16
  830.3 32.1 %fusion.149 = bf16[900,3072]{1,0:T(8,128)(2,1)} fusion(f32[3072]{0:T(1024)S(1)} %convert_element_type.95, bf16[3072,1,768]{2,1,0:T(2,128)(2,1)S(1)} %get-tuple-element.5, f32[1,900,768]{2,1,0:T(8,128)} %copy-done.1, f32[768]{0:T(1024)S(1)} %copy-done.14, f32[768]{0:T(1024)S(1)} %copy-done.15, f32[900]{0:T(1024)S(1)} %add_rsqrt_fusion, ...), kind=kOutput, calls=%fused_computation.3.clone.clone.clone.clone.1 | convolution fusion | flops 4432665600 | bytes 13038624 | tf_op jit(solution)/shard_map/dot_general | solution.py:134
  862.3 0.0 copy-done.2
  862.4 0.0 copy-done.16
  862.4 6.6 bitcast_add_fusion
  869.0 4.4 copy.122
  (36 shorter events, 0.1 us)
Async XLA Ops:
  6.5 9.2 %copy-start = (f32[1,900,768]{2,0,1:T(1,128)S(1)}, f32[1,900,768]{2,0,1:T(1,128)}, u32[]{:S(2)}) copy-start(f32[1,900,768]{2,0,1:T(1,128)} %param.12) | copy-start | bytes 8294404
  6.5 805.2 %all-gather.2.cloned.1.call-start = ((), (), s32[]{:S(2)}) async-start(), calls=%async_computation.4 | async-start | bytes 9474048 | tf_op jit(solution)/shard_map/all_gather | solution.py:132
  12.0 4.3 copy-start.12
  12.0 4.3 copy-start.13
  93.0 6.6 copy-start.8
  93.0 6.8 copy-start.9
  93.0 27.3 %all-to-all-start.1 = ((f32[8,1,49152]{2,1,0:T(1,128)}), f32[8,1,49152]{2,1,0:T(1,128)}, u32[]{:S(2)}, u32[]{:S(2)}) async-start(f32[8,1,49152]{2,1,0:T(1,128)} %reshape.513), calls=%async_computation.1 | async-start | bytes 3145728 | tf_op jit(solution)/shard_map/all_to_all | solution.py:72
  142.8 8.6 copy-start.10
  148.4 6.0 copy-start.11
  151.5 3.0 copy-start.6
  151.5 3.0 copy-start.7
  151.5 5.1 copy-start.3
  224.4 8.1 copy-start.17
  227.2 95.0 %all-to-all-start.3 = ((f32[8,2,256,96]{2,3,1,0:T(8,128)}), f32[8,2,256,96]{2,3,1,0:T(8,128)}, u32[]{:S(2)}, u32[]{:S(2)}) async-start(f32[8,2,256,96]{2,3,1,0:T(8,128)} %copy.116), calls=%async_computation.3 | async-start | bytes 3145728 | tf_op jit(solution)/shard_map/all_to_all | solution.py:113
  322.1 1.7 copy-start.4
  322.1 1.9 copy-start.5
  329.4 1.5 copy-start.1
  331.4 498.9 %copy-start.14 = (f32[768]{0:T(1024)S(1)}, f32[768]{0:T(1024)}, u32[]{:S(2)}) copy-start(f32[768]{0:T(1024)} %param.20) | copy-start | bytes 9220
  331.4 498.9 %copy-start.15 = (f32[768]{0:T(1024)S(1)}, f32[768]{0:T(1024)}, u32[]{:S(2)}) copy-start(f32[768]{0:T(1024)} %param.19) | copy-start | bytes 9220
  830.2 32.1 %copy-start.2 = (f32[1,900,768]{2,1,0:T(8,128)S(1)}, f32[1,900,768]{2,1,0:T(8,128)}, u32[]{:S(2)}) copy-start(f32[1,900,768]{2,1,0:T(8,128)} %copy-done.1) | copy-start | bytes 8294404
  830.2 32.1 %copy-start.16 = (f32[768]{0:T(1024)S(1)}, f32[768]{0:T(1024)}, u32[]{:S(2)}) copy-start(f32[768]{0:T(1024)} %param.23) | copy-start | bytes 9220
Sparse Core Ops, SparseCore 0:
  9.2 802.5 all-gather.1
where the time goes:
time: 890 us; the launch traced here: 880 us
  waiting for transfers between devices  496 us (56%)
  blocking collectives  190 us (21%)
  local copies, waits for them, and re-layouts  77.1 us (9%)
  matrix products  64.9 us (7%)
  other arithmetic  27 us (3%)
  between operations  14 us (2%)
  starting transfers between devices  11.9 us (1%)
    all_gather x1, waiting for transfers between devices, per_device(): lax.all_gather(dense_weights, ('lat', 'chan'), axis=0, tiled=True)  480 us
    unnamed x1, blocking collectives  84.4 us
    all_to_all x1, blocking collectives, per_device(): lax.all_to_all(lat_back, 'lat', split_axis=0, concat_axis=2, tiled=True)  56.5 us
    all_to_all x1, blocking collectives, per_device(): lax.all_to_all(lon_modes, 'lat', split_axis=2, concat_axis=0, tiled=True)  49 us
    dot_general x1, matrix products, per_device(): lax.dot_general(flat_normed, weight_block[:, 0, :], (((1,), (1,)), ((), (...  32.1 us
    unnamed x45, local copies, waits for them, and re-layouts  22.1 us
    slice x1, local copies, waits for them, and re-layouts, per_device(): weight_block[:, 0, :]  18.4 us
  transfers between devices with their start and end apart: 3, of which 2 were waited for; matrix products, arithmetic and copies ran while one was open for 12% of the time, Pallas kernels for 0%

commit v1 on v0

--- a/solution.py
+++ b/solution.py
@@ -129,7 +129,8 @@
         .astype(jnp.bfloat16)
         .reshape(token_count, channels)
     )
-    weight_block = lax.all_gather(dense_weights, ("lat", "chan"), axis=0, tiled=True)
+    outgoing = jnp.stack([dense_weights] * lax.axis_size(("lat", "chan")))
+    weight_block = jnp.concatenate(lax.all_to_all(outgoing, ("lat", "chan"), 0, 0), axis=0)
     bias_block = lax.all_gather(dense_bias, ("lat", "chan"), axis=0, tiled=True)
     pre_act = lax.dot_general(
         flat_normed,

time: 890 us -> 595 us (0.67)
  the two profiles are of different devices: /device:TPU:99 before, /device:TPU:1 now
where the time goes in v1:
time: 595 us; the launch traced here: 586 us
  blocking collectives  382 us (64%)
  local copies, waits for them, and re-layouts  82.6 us (14%)
  matrix products  64.2 us (11%)
  other arithmetic  26.8 us (5%)
  waiting for transfers between devices  14.5 us (2%)
  starting transfers between devices  14.3 us (2%)
    unnamed x1, blocking collectives  249 us
    all_to_all x1, blocking collectives, per_device(): lax.all_to_all(lon_modes, 'lat', split_axis=2, concat_axis=0, tiled=True)  52.8 us
    all_to_all x1, blocking collectives, per_device(): lax.all_to_all(lat_back, 'lat', split_axis=0, concat_axis=2, tiled=True)  46.3 us
    all_to_all x1, blocking collectives, per_device(): lax.all_to_all(lax.all_to_all(lat_back, 'lat', split_axis=0, concat_axis=...  33.8 us
    dot_general x1, matrix products, per_device(): lax.dot_general(flat_normed, weight_block[:, 0, :], (((1,), (1,)), ((), (...  31.9 us
    unnamed x49, local copies, waits for them, and re-layouts  22.8 us
    slice x1, local copies, waits for them, and re-layouts, per_device(): weight_block[:, 0, :]  18.4 us
    all_to_all x1, waiting for transfers between devices, per_device(): lax.all_to_all(lax.all_to_all(lon_modes, 'lat', split_axis=2, concat_axis...  14.5 us
  transfers between devices with their start and end apart: 2, of which 1 were waited for; matrix products, arithmetic and copies ran while one was open for 3% of the time, Pallas kernels for 0%

profile of v1, /device:TPU:1, one launch (start us, length us, event | category | flops | bytes accessed | tf_op | source)
XLA Modules:
  0.0 585.7 jit_solution(6098489927003370731)
XLA Ops:
  0.0 4.8 sine_negate_fusion
  4.8 4.6 reduce_sum.36
  9.4 0.0 copy-start.5
  9.4 0.0 copy-start.6
  9.4 0.0 copy-done
  9.4 0.4 multiply_reduce_fusion.1
  9.9 0.7 copy-done.5
  10.6 0.3 copy-done.6
  10.9 5.9 %fusion.44 = f32[1,2,256,768]{3,2,1,0:T(8,128)S(1)} fusion(f32[1,900,768]{2,0,1:T(1,128)S(1)} %copy-done, f32[900,1,256]{2,0,1:T(8,128)S(1)} %copy-done.5, f32[900,1,256]{2,0,1:T(8,128)S(1)} %copy-done.6, f32[768]{0:T(1024)S(1)} %copy-done.14, f32[768]{0:T(1024)S(1)} %copy-done.15, f32[900]{0:T(1024)S(1)} %add_rsqrt_fusion.1, ...), kind=kOutput, calls=%fused_computation.54 | convolution fusion | flops 4250419200 | bytes 6194208 | tf_op jit(solution)/shard_map/rwc,wak->rakc/dot_general | solution.py:71
  16.8 1.2 copy.103
  18.0 52.8 %all_to_all.71 = f32[1,2,256,768]{3,1,0,2:T(2,128)} all-to-all(f32[1,2,256,768]{3,1,0,2:T(2,128)S(1)} %copy.103), channel_id=1, replica_groups=mesh['lat'=32,'chan'=8] {'lat'}, dimensions={2} | all-to-all | bytes 3145728 | tf_op jit(solution)/shard_map/all_to_all | solution.py:73
  70.8 6.5 %copy.104 = f32[1,2,32,8,768]{2,3,1,4,0:T(8,128)} copy(f32[1,2,32,8,768]{4,1,3,2,0:T(2,128)} %bitcast.157) | data formatting | bytes 3145728 | tf_op jit(solution)/shard_map/all_to_all | solution.py:73
  77.3 5.8 bitcast_bitcast_fusion
  83.2 7.6 %reshape.519 = f32[8,1,49152]{2,1,0:T(1,128)} reshape(f32[768,2,8,32]{3,2,1,0:T(8,128)} %bitcast_bitcast_fusion) | data formatting | bytes 3145728
  90.8 5.0 all-to-all-start.1
  95.8 0.0 copy-done.9
  95.8 0.1 copy.132
  95.9 0.1 copy.131
  96.1 0.1 copy.130
  96.1 0.1 copy.129
  96.3 0.7 maximum_bitcast_fusion.8
  97.0 1.0 fusion.102
  98.0 1.0 fusion.98
  99.0 1.0 fusion.103
  100.1 1.1 maximum_bitcast_fusion.2
  101.1 0.9 maximum_bitcast_fusion
  102.0 14.5 %all-to-all-done.1 = f32[8,1,49152]{2,1,0:T(1,128)} async-done(((f32[8,1,49152]{2,1,0:T(1,128)}), f32[8,1,49152]{2,1,0:T(1,128)}, u32[]{:S(2)}, u32[]{:S(2)}) %all-to-all-start.1) | async-done | bytes 1572896 | tf_op jit(solution)/shard_map/all_to_all | solution.py:72
  116.5 0.6 broadcast.665
  117.1 6.9 %reduce.4 = f32[8,49152]{1,0:T(8,128)} reduce(f32[8,1,49152]{2,1,0:T(1,128)} %all-to-all-done.1, f32[]{:T(128)} %broadcast.665), dimensions={1}, to_apply=%all_to_all.55.reduce_sub_computation | reduce | bytes 3145732 | tf_op jit(solution)/shard_map/all_to_all | solution.py:72
  124.0 6.1 %reshape.520 = f32[768,2,8,32]{3,2,1,0:T(8,128)} reshape(f32[8,49152]{1,0:T(8,128)} %reduce.4) | data formatting | bytes 3145728
  130.1 5.9 %copy.105 = f32[32,2,8,8,96]{4,2,0,3,1:T(8,128)} copy(f32[32,2,8,8,96]{0,2,1,4,3:T(8,128)} %bitcast.150) | data formatting | bytes 3145728 | tf_op jit(solution)/shard_map/all_to_all | solution.py:72
  136.0 3.3 reshape.507
  139.3 0.0 copy-start.12
  139.3 5.6 convolution_bitcast_fusion.1
  144.9 3.1 copy.106
  148.0 3.0 fusion.39
  151.0 2.0 maximum_multiply_fusion.2
  153.1 3.9 convolution_bitcast_fusion
  156.9 3.0 copy.110
  160.0 2.9 copy.111
  162.9 46.3 %all_to_all.72 = f32[256,2,8,96]{3,2,1,0:T(8,128)S(1)} all-to-all(f32[256,2,8,96]{3,2,1,0:T(8,128)} %copy.111), channel_id=1, replica_groups=mesh['lat'=32,'chan'=8] {'lat'}, dimensions={0} | all-to-all | bytes 3145728 | tf_op jit(solution)/shard_map/all_to_all | solution.py:114
  209.2 1.5 copy.179
  210.7 2.8 copy.113
  213.6 33.8 %all_to_all.73 = f32[8,2,256,96]{2,3,1,0:T(8,128)} all-to-all(f32[8,2,256,96]{2,3,1,0:T(8,128)} %copy.113), channel_id=1, replica_groups=mesh['lat'=32,'chan'=8] {'chan'}, dimensions={0} | all-to-all | bytes 3145728 | tf_op jit(solution)/shard_map/all_to_all | solution.py:113
  247.3 0.0 copy-done.11
  247.3 6.2 %stack.68 = bf16[256,12,2,768]{3,2,1,0:T(2,128)(2,1)} broadcast(bf16[12,2,768]{2,1,0:T(2,128)(2,1)S(1)} %copy-done.11), dimensions={1,2,3} | broadcast | bytes 9474048 | tf_op jit(solution)/shard_map/stack | solution.py:132
  253.5 9.3 %all-to-all-start.4 = ((bf16[256,12,2,768]{3,2,1,0:T(2,128)(2,1)}), bf16[256,12,2,768]{3,2,1,0:T(2,128)(2,1)}, u32[]{:S(2)}, u32[]{:S(2)}) async-start(bf16[256,12,2,768]{3,2,1,0:T(2,128)(2,1)} %stack.68), calls=%async_computation.4 | async-start | bytes 18874368 | tf_op jit(solution)/shard_map/all_to_all | solution.py:133
  262.9 0.2 dynamic-update-slice
  263.1 249.4 %all-reduce = bf16[3072]{0:T(1024)(128)(2,1)S(1)} all-reduce(bf16[3072]{0:T(1024)(128)(2,1)S(1)} %dynamic-update-slice), channel_id=1, replica_groups=mesh['lat'=32,'chan'=8] {'lat','chan'}, use_global_device_ids=true, to_apply=%add | all-reduce | flops 3072 | bytes 12288
  512.5 3.8 cosine_multiply_fusion
  516.4 0.1 copy.114
  516.5 5.3 fusion.150
  521.8 1.6 copy-done.2
  523.3 0.5 multiply_reduce_fusion
  523.8 0.0 all-to-all-done.4
  523.8 0.0 copy-start.16
  523.8 0.0 copy-start.17
  523.9 18.4 %fusion.147 = (bf16[3072,1,768]{2,1,0:T(2,128)(2,1)S(1)}, bf16[3072,1,768]{2,1,0:T(2,128)(2,1)S(1)}) fusion(bf16[3072,2,768]{2,1,0:T(2,128)(2,1)} %bitcast.57), kind=kLoop, calls=%fused_computation.183 | loop fusion | bytes 18874368 | tf_op jit(solution)/shard_map/slice | solution.py:137
  542.3 0.0 copy-start.18
  542.3 31.9 %fusion.163 = bf16[900,3072]{1,0:T(8,128)(2,1)} fusion(f32[3072]{0:T(1024)S(1)} %convert_element_type.95, bf16[3072,1,768]{2,1,0:T(2,128)(2,1)S(1)} %get-tuple-element.5, f32[1,900,768]{2,1,0:T(8,128)} %copy-done.2, f32[768]{0:T(1024)S(1)} %copy-done.16, f32[768]{0:T(1024)S(1)} %copy-done.17, f32[900]{0:T(1024)S(1)} %add_rsqrt_fusion, ...), kind=kOutput, calls=%fused_computation.3.clone.clone.clone.clone.1 | convolution fusion | flops 4432665600 | bytes 13038624 | tf_op jit(solution)/shard_map/dot_general | solution.py:135
  574.2 0.0 copy-done.3
  574.2 0.0 copy-done.18
  574.2 6.6 %bitcast_add_fusion = f32[1,900,768]{2,1,0:T(8,128)S(1)} fusion(f32[1,900,768]{2,1,0:T(8,128)S(1)} %copy-done.3, bf16[3072,1,768]{2,1,0:T(2,128)(2,1)S(1)} %get-tuple-element.6, f32[768]{0:T(1024)S(1)} %copy-done.18, bf16[900,3072]{1,0:T(8,128)(2,1)} %fusion.163), kind=kOutput, calls=%fused_computation.25 | convolution fusion | flops 4248115200 | bytes 15780864 | tf_op jit(solution)/shard_map/dot_general | solution.py:142
  580.9 4.4 copy.117
  (39 shorter events, 0.1 us)
Async XLA Ops:
  0.0 9.4 %copy-start = (f32[1,900,768]{2,0,1:T(1,128)S(1)}, f32[1,900,768]{2,0,1:T(1,128)}, u32[]{:S(2)}) copy-start(f32[1,900,768]{2,0,1:T(1,128)} %param.12) | copy-start | bytes 8294404
  4.8 5.1 copy-start.14
  4.8 5.1 copy-start.15
  9.4 1.2 copy-start.5
  9.4 1.5 copy-start.6
  90.8 5.0 copy-start.9
  90.8 5.2 copy-start.10
  90.8 25.7 %all-to-all-start.1 = ((f32[8,1,49152]{2,1,0:T(1,128)}), f32[8,1,49152]{2,1,0:T(1,128)}, u32[]{:S(2)}, u32[]{:S(2)}) async-start(f32[8,1,49152]{2,1,0:T(1,128)} %reshape.519), calls=%async_computation.1 | async-start | bytes 3145728 | tf_op jit(solution)/shard_map/all_to_all | solution.py:72
  139.3 8.7 %copy-start.12 = (f32[1,2,96]{2,1,0:T(2,128)S(1)}, f32[1,2,96]{2,1,0:T(2,128)}, u32[]{:S(2)}) copy-start(f32[1,2,96]{2,1,0:T(2,128)} %param.16) | copy-start | bytes 2308
  144.9 6.1 %copy-start.13 = (f32[1,2,96]{2,1,0:T(2,128)S(1)}, f32[1,2,96]{2,1,0:T(2,128)}, u32[]{:S(2)}) copy-start(f32[1,2,96]{2,1,0:T(2,128)} %param.18) | copy-start | bytes 2308
  148.0 3.0 copy-start.7
  148.0 3.0 copy-start.8
  148.0 5.1 copy-start.4
  210.7 36.6 %copy-start.11 = (bf16[12,2,768]{2,1,0:T(2,128)(2,1)S(1)}, bf16[12,2,768]{2,1,0:T(2,128)(2,1)}, u32[]{:S(2)}) copy-start(bf16[12,2,768]{2,1,0:T(2,128)(2,1)} %param.21) | copy-start | bytes 110596
  253.5 9.4 %copy-start.19 = (bf16[12]{0:T(256)(128)(2,1)S(1)}, bf16[12]{0:T(256)(128)(2,1)}, u32[]{:S(2)}) copy-start(bf16[12]{0:T(256)(128)(2,1)} %param.22) | copy-start | bytes 76
  253.5 270.3 %all-to-all-start.4 = ((bf16[256,12,2,768]{3,2,1,0:T(2,128)(2,1)}), bf16[256,12,2,768]{3,2,1,0:T(2,128)(2,1)}, u32[]{:S(2)}, u32[]{:S(2)}) async-start(bf16[256,12,2,768]{3,2,1,0:T(2,128)(2,1)} %stack.68), calls=%async_computation.4 | async-start | bytes 18874368 | tf_op jit(solution)/shard_map/all_to_all | solution.py:133
  512.5 3.8 copy-start.1
  521.8 1.6 copy-start.2
  523.8 18.4 %copy-start.16 = (f32[768]{0:T(1024)S(1)}, f32[768]{0:T(1024)}, u32[]{:S(2)}) copy-start(f32[768]{0:T(1024)} %param.20) | copy-start | bytes 9220
  523.8 18.4 %copy-start.17 = (f32[768]{0:T(1024)S(1)}, f32[768]{0:T(1024)}, u32[]{:S(2)}) copy-start(f32[768]{0:T(1024)} %param.19) | copy-start | bytes 9220
  542.3 31.9 %copy-start.3 = (f32[1,900,768]{2,1,0:T(8,128)S(1)}, f32[1,900,768]{2,1,0:T(8,128)}, u32[]{:S(2)}) copy-start(f32[1,900,768]{2,1,0:T(8,128)} %copy-done.2) | copy-start | bytes 8294404
  542.3 31.9 %copy-start.18 = (f32[768]{0:T(1024)S(1)}, f32[768]{0:T(1024)}, u32[]{:S(2)}) copy-start(f32[768]{0:T(1024)} %param.23) | copy-start | bytes 9220
